TPU v7x, 32 devices: a whole 2x2x4 slice. The times are simulated.
32 devices in a mesh: expert: 4 (over z), seq: 4 (over y, x), dp: 2 (over core).
Axes of the slice: x: 2, y: 2, z: 4, core: 2. Of those that a mesh axis runs over, the one named last changes fastest.
Arguments:
- grad_out: bfloat16 [8, 512, 2048], P(('expert', 'dp'), 'seq'), may hold values from -6 to 6
- expert_ids: int32 [8, 512, 2], P(('expert', 'dp'), 'seq'), may hold values from 0 to 3, all different within a row; in each aligned block of 128 rows (0 to 127, 128 to 255, ..., all dimensions but the last counted through in order) at most 112 rows name the same one
- gate_weights: float32 [8, 512, 2], P(('expert', 'dp'), 'seq'), may hold values from 0.1 to 0.9
- hidden: bfloat16 [8, 512, 2, 7168], P(('expert', 'dp'), 'seq'), may hold values from -0.3125 to 0.3125
- queries: bfloat16 [8, 512, 2048], P(('expert', 'dp'), 'seq')
- keys: bfloat16 [8, 512, 512], P(('expert', 'dp'), 'seq')
- values: bfloat16 [8, 512, 512], P(('expert', 'dp'), 'seq'), may hold values from -6 to 6
Outputs:
- expert_grad: bfloat16 [4, 7168, 2048], P('expert', ('seq', 'dp'))
- grad_queries: bfloat16 [8, 512, 2048], P(('expert', 'dp'), 'seq')
- grad_keys: bfloat16 [8, 512, 512], P(('expert', 'dp'), 'seq')
- grad_values: bfloat16 [8, 512, 512], P(('expert', 'dp'), 'seq')
Inputs may be any that keep to these rules, and one draw needn't show every extreme that they name: `expert_ids`: each position names two different experts; among the 128 positions of one device no expert is named more than 112 times.
All inputs are finite; a program needn't handle non-finite values.
Results may differ from a plain program's by a relative error of at most 0.018.
Values may be sent and summed in bfloat16 or wider, within the bound.
A program may use at most 128 MiB of HBM per device.

v0:
```python
import jax
import jax.numpy as jnp
from jax import lax
from jax.sharding import PartitionSpec as P

HEADS = 16
KV_HEADS = 4
HEAD_DIM = 128


def expert_grads(grad_out, expert_ids, gate_weights, hidden):
    experts = lax.axis_size("expert")
    shards = lax.axis_size("seq")
    pair_size = lax.axis_size("dp")
    tokens = grad_out.shape[1]
    model_width = grad_out.shape[2]
    unit_piece = hidden.shape[3] // shards
    owner_piece = unit_piece // pair_size
    row_count = tokens * 2
    capacity = 7 * tokens // (2 * experts)
    flat_ids = expert_ids.reshape(row_count)
    scaled = (gate_weights[0][..., None] * grad_out[0][:, None, :].astype(jnp.float32)).astype(
        jnp.bfloat16
    )
    scaled = scaled.reshape(row_count, model_width)
    onehot = (flat_ids[:, None] == jnp.arange(experts, dtype=jnp.int32)[None, :]).astype(jnp.int32)
    before = jnp.cumsum(onehot, axis=0) - onehot
    slot_index = jnp.sum(before * onehot, axis=1)
    flat_hidden = hidden.reshape(row_count, shards, unit_piece)
    hidden_send = jnp.zeros((experts, shards, capacity, unit_piece), jnp.bfloat16)
    hidden_send = hidden_send.at[flat_ids, :, slot_index, :].set(flat_hidden)
    spread = jnp.broadcast_to(scaled[:, None, :], (row_count, shards, model_width))
    grad_send = jnp.zeros((experts, shards, capacity, model_width), jnp.bfloat16)
    grad_send = grad_send.at[flat_ids, :, slot_index, :].set(spread)
    grad_recv, hidden_recv = (
        lax.all_to_all(
            grad_send.reshape(experts * shards, capacity, model_width),
            ("expert", "seq"),
            split_axis=0,
            concat_axis=0,
            tiled=True,
        ),
        lax.all_to_all(
            hidden_send.reshape(experts * shards, capacity, unit_piece),
            ("expert", "seq"),
            split_axis=0,
            concat_axis=0,
            tiled=True,
        ),
    )
    grad_rows = grad_recv.reshape(-1, model_width)
    hidden_rows = hidden_recv.reshape(-1, unit_piece)
    local_grad = lax.psum_scatter(
        lax.dot_general(
            hidden_rows, grad_rows, (((0,), (0,)), ((), ())), preferred_element_type=jnp.float32
        ).astype(jnp.bfloat16),
        "dp",
        scatter_dimension=0,
        tiled=True,
    )
    return local_grad.reshape(1, owner_piece, model_width)


def attention_grads(queries, keys, values, grad_out):
    per_group = HEADS // KV_HEADS
    score_scale = HEAD_DIM ** (-0.5)
    tokens = queries.shape[1]
    whole_keys, whole_values = (
        lax.all_gather(keys, "seq", axis=1, tiled=True),
        lax.all_gather(values, "seq", axis=1, tiled=True),
    )
    key_count = whole_keys.shape[1]
    query_heads = queries[0].reshape(tokens, KV_HEADS, per_group, HEAD_DIM)
    out_heads = grad_out[0].reshape(tokens, KV_HEADS, per_group, HEAD_DIM)
    key_heads = whole_keys[0].reshape(key_count, KV_HEADS, HEAD_DIM)
    value_heads = whole_values[0].reshape(key_count, KV_HEADS, HEAD_DIM)
    scores = (
        jnp.einsum("qhgd,khd->hgqk", query_heads, key_heads, preferred_element_type=jnp.float32)
        * score_scale
    )
    row_max = jnp.max(scores, axis=-1, keepdims=True)
    raised = jnp.exp(scores - row_max)
    probabilities = raised / jnp.sum(raised, axis=-1, keepdims=True)
    probs_low = probabilities.astype(jnp.bfloat16)
    dprobs = jnp.einsum(
        "qhgd,khd->hgqk", out_heads, value_heads, preferred_element_type=jnp.float32
    )
    row_delta = jnp.sum(probabilities * dprobs, axis=-1, keepdims=True)
    dscores = (probabilities * (dprobs - row_delta)).astype(jnp.bfloat16)
    value_part = jnp.einsum(
        "hgqk,qhgd->khd", probs_low, out_heads, preferred_element_type=jnp.float32
    )
    key_part = (
        jnp.einsum("hgqk,qhgd->khd", dscores, query_heads, preferred_element_type=jnp.float32)
        * score_scale
    )
    grad_q = (
        jnp.einsum("hgqk,khd->qhgd", dscores, key_heads, preferred_element_type=jnp.float32)
        * score_scale
    )
    key_sums, value_sums = (
        lax.psum_scatter(
            key_part.reshape(1, key_count, KV_HEADS * HEAD_DIM).astype(jnp.bfloat16),
            "seq",
            scatter_dimension=1,
            tiled=True,
        ).astype(jnp.float32),
        lax.psum_scatter(
            value_part.reshape(1, key_count, KV_HEADS * HEAD_DIM).astype(jnp.bfloat16),
            "seq",
            scatter_dimension=1,
            tiled=True,
        ).astype(jnp.float32),
    )
    grad_queries = grad_q.reshape(1, tokens, HEADS * HEAD_DIM).astype(jnp.bfloat16)
    return (grad_queries, key_sums.astype(jnp.bfloat16), value_sums.astype(jnp.bfloat16))


def on_device(grad_out, expert_ids, gate_weights, hidden, queries, keys, values):
    expert_grad = expert_grads(grad_out, expert_ids, gate_weights, hidden)
    grad_queries, grad_keys, grad_values = attention_grads(queries, keys, values, grad_out)
    return (expert_grad, grad_queries, grad_keys, grad_values)


def solution(mesh):
    in_specs = (
        P(("expert", "dp"), "seq", None),
        P(("expert", "dp"), "seq", None),
        P(("expert", "dp"), "seq", None),
        P(("expert", "dp"), "seq", None, None),
        P(("expert", "dp"), "seq", None),
        P(("expert", "dp"), "seq", None),
        P(("expert", "dp"), "seq", None),
    )
    out_specs = (
        P("expert", ("seq", "dp"), None),
        P(("expert", "dp"), "seq", None),
        P(("expert", "dp"), "seq", None),
        P(("expert", "dp"), "seq", None),
    )
    return jax.shard_map(
        on_device, mesh=mesh, in_specs=in_specs, out_specs=out_specs, check_vma=False
    )
```

profile of v0, /device:TPU:0, one launch (start us, length us, event | category | flops | bytes accessed | tf_op | source)
XLA Modules:
  0.0 443.8 jit_solution(10077372838262434562)
XLA Ops:
  10.0 9.8 %reshape.163 = bf16[256,4,1792]{2,1,0:T(4,128)(2,1)} reshape(bf16[1,128,2,7168]{3,2,1,0:T(2,128)(2,1)} %param.10) | data formatting | bytes 7340032 | tf_op jit(solution)/shard_map/reshape | solution.py:29
  19.8 4.3 broadcast_in_dim.6
  24.2 36.0 %scatter_fusion = bf16[4,4,112,1792]{3,1,2,0:T(4,128)(2,1)} fusion(bf16[4,4,112,1792]{3,1,2,0:T(4,128)(2,1)} %broadcast_in_dim.6, s32[256]{0:T(256)S(1)} %bitcast.98, bf16[256,4,1792]{2,1,0:T(4,128)(2,1)} %reshape.163), kind=kCustom, calls=%fused_computation | custom fusion | bytes 11012096 | tf_op jit(solution)/shard_map/scatter | solution.py:31
  60.2 6.3 %copy.31 = bf16[4,4,112,1792]{3,2,1,0:T(8,128)(2,1)} copy(bf16[4,4,112,1792]{3,1,2,0:T(4,128)(2,1)} %scatter_fusion) | data formatting | bytes 12845056 | tf_op jit(solution)/shard_map/scatter | solution.py:31
  66.5 8.5 %all-to-all-start = ((bf16[16,112,1792]{2,1,0:T(8,128)(2,1)}), bf16[16,112,1792]{2,1,0:T(8,128)(2,1)}, u32[]{:S(2)}, u32[]{:S(2)}) async-start(bf16[16,112,1792]{2,1,0:T(8,128)(2,1)} %bitcast.101), calls=%async_computation | async-start | bytes 12845056 | tf_op jit(solution)/shard_map/all_to_all | solution.py:43
  75.2 2.5 mul.56
  77.7 2.7 mul.57
  80.8 4.2 broadcast_in_dim.8
  85.1 6.7 %broadcast_in_dim.7 = bf16[4,4,112,2048]{3,1,2,0:T(4,128)(2,1)} broadcast(bf16[]{:T(256)} %constant.7.clone.1), dimensions={} | broadcast | bytes 7340034 | tf_op jit(solution)/shard_map/broadcast_in_dim | solution.py:33
  91.8 36.4 %scatter_fusion.1 = bf16[4,4,112,2048]{3,1,2,0:T(4,128)(2,1)} fusion(bf16[4,4,112,2048]{3,1,2,0:T(4,128)(2,1)} %broadcast_in_dim.7, s32[256]{0:T(256)S(1)} %bitcast.99, bf16[256,4,2048]{2,1,0:T(4,128)(2,1)} %broadcast_in_dim.8), kind=kCustom, calls=%fused_computation.1 | custom fusion | bytes 12584960 | tf_op jit(solution)/shard_map/scatter | solution.py:34
  128.1 10.2 %copy.33 = bf16[4,4,112,2048]{3,2,1,0:T(8,128)(2,1)} copy(bf16[4,4,112,2048]{3,1,2,0:T(4,128)(2,1)} %scatter_fusion.1) | data formatting | bytes 14680064 | tf_op jit(solution)/shard_map/scatter | solution.py:34
  138.3 57.2 %all-to-all-done = bf16[16,112,1792]{2,1,0:T(8,128)(2,1)} async-done(((bf16[16,112,1792]{2,1,0:T(8,128)(2,1)}), bf16[16,112,1792]{2,1,0:T(8,128)(2,1)}, u32[]{:S(2)}, u32[]{:S(2)}) %all-to-all-start) | async-done | bytes 6422560 | tf_op jit(solution)/shard_map/all_to_all | solution.py:43
  195.5 30.8 %all-to-all-start.1 = ((bf16[16,112,2048]{2,1,0:T(8,128)(2,1)}), bf16[16,112,2048]{2,1,0:T(8,128)(2,1)}, u32[]{:S(2)}, u32[]{:S(2)}) async-start(bf16[16,112,2048]{2,1,0:T(8,128)(2,1)} %bitcast.100), calls=%async_computation.1 | async-start | bytes 14680064 | tf_op jit(solution)/shard_map/all_to_all | solution.py:36
  227.2 48.6 %all_gather.6 = bf16[1,512,512]{1,2,0:T(8,128)(2,1)S(1)} all-gather(bf16[1,128,512]{1,2,0:T(8,128)(2,1)S(1)} %copy.34), channel_id=1, replica_groups=mesh['expert'=4,'seq'=4,'dp'=2] {'seq'}, dimensions={1}, use_global_device_ids=true | all-gather | bytes 655360 | tf_op jit(solution)/shard_map/all_gather | solution.py:69
  275.8 18.1 %all_gather.7 = bf16[1,512,512]{1,2,0:T(8,128)(2,1)S(1)} all-gather(bf16[1,128,512]{1,2,0:T(8,128)(2,1)S(1)} %copy.37), channel_id=1, replica_groups=mesh['expert'=4,'seq'=4,'dp'=2] {'seq'}, dimensions={1}, use_global_device_ids=true | all-gather | bytes 655360 | tf_op jit(solution)/shard_map/all_gather | solution.py:70
  293.9 3.4 fusion.28
  297.4 3.1 fusion.1
  303.5 2.1 copy.43
  305.6 3.8 fusion.18
  309.5 2.1 copy.46
  311.6 49.2 %all-to-all-done.1 = bf16[16,112,2048]{2,1,0:T(8,128)(2,1)} async-done(((bf16[16,112,2048]{2,1,0:T(8,128)(2,1)}), bf16[16,112,2048]{2,1,0:T(8,128)(2,1)}, u32[]{:S(2)}, u32[]{:S(2)}) %all-to-all-start.1) | async-done | bytes 7340064 | tf_op jit(solution)/shard_map/all_to_all | solution.py:36
  360.8 19.6 %bitcast_convert_fusion = bf16[1792,2048]{1,0:T(8,128)(2,1)} fusion(bf16[16,112,1792]{2,1,0:T(8,128)(2,1)} %all-to-all-done, bf16[16,112,2048]{2,1,0:T(8,128)(2,1)} %all-to-all-done.1), kind=kOutput, calls=%fused_computation.3 | convolution fusion | flops 13157007360 | bytes 21102592 | tf_op jit(solution)/shard_map/dot_general | solution.py:54
  382.0 36.6 %reduce-scatter.8.cloned.1.call-done = bf16[1,128,512]{2,1,0:T(8,128)(2,1)} async-done(((bf16[1,512,512]{2,1,0:T(8,128)(2,1)}), bf16[1,128,512]{2,1,0:T(8,128)(2,1)}) %reduce-scatter.8.cloned.1.call-update) | async-done | bytes 131088 | tf_op jit(solution)/shard_map/reduce_scatter | solution.py:108
  418.5 18.7 %reduce-scatter.4.cloned.1.call-done = bf16[896,2048]{1,0:T(8,128)(2,1)} async-done(((bf16[1792,2048]{1,0:T(8,128)(2,1)}), bf16[896,2048]{1,0:T(8,128)(2,1)}) %reduce-scatter.4.cloned.1.call-update) | async-done | bytes 3670032 | tf_op jit(solution)/shard_map/reduce_scatter | solution.py:53
  (49 shorter events, 8.8 us)
Async XLA Ops:
  66.5 8.5 %copy-start.1 = (bf16[1,128,2048]{2,1,0:T(8,128)(2,1)S(1)}, bf16[1,128,2048]{2,1,0:T(8,128)(2,1)}, u32[]{:S(2)}) copy-start(bf16[1,128,2048]{2,1,0:T(8,128)(2,1)} %param.7) | copy-start | bytes 1572868
  66.5 129.0 %all-to-all-start = ((bf16[16,112,1792]{2,1,0:T(8,128)(2,1)}), bf16[16,112,1792]{2,1,0:T(8,128)(2,1)}, u32[]{:S(2)}, u32[]{:S(2)}) async-start(bf16[16,112,1792]{2,1,0:T(8,128)(2,1)} %bitcast.101), calls=%async_computation | async-start | bytes 12845056 | tf_op jit(solution)/shard_map/all_to_all | solution.py:43
  75.0 5.3 %copy-start.7 = (f32[1,128,2]{1,2,0:T(2,128)S(1)}, f32[1,128,2]{1,2,0:T(2,128)}, u32[]{:S(2)}) copy-start(f32[1,128,2]{1,2,0:T(2,128)} %param.9) | copy-start | bytes 3076
  195.5 31.1 %copy-start.5 = (bf16[1,128,512]{2,1,0:T(8,128)(2,1)S(1)}, bf16[1,128,512]{2,1,0:T(8,128)(2,1)}, u32[]{:S(2)}) copy-start(bf16[1,128,512]{2,1,0:T(8,128)(2,1)} %param.12) | copy-start | bytes 393220
  195.5 31.2 %copy-start.2 = (bf16[1,128,2048]{2,1,0:T(8,128)(2,1)S(1)}, bf16[1,128,2048]{2,1,0:T(8,128)(2,1)}, u32[]{:S(2)}) copy-start(bf16[1,128,2048]{2,1,0:T(8,128)(2,1)} %param.11) | copy-start | bytes 1572868
  195.5 31.5 %copy-start.6 = (bf16[1,128,512]{2,1,0:T(8,128)(2,1)S(1)}, bf16[1,128,512]{2,1,0:T(8,128)(2,1)}, u32[]{:S(2)}) copy-start(bf16[1,128,512]{2,1,0:T(8,128)(2,1)} %param.13) | copy-start | bytes 393220
  195.5 165.3 %all-to-all-start.1 = ((bf16[16,112,2048]{2,1,0:T(8,128)(2,1)}), bf16[16,112,2048]{2,1,0:T(8,128)(2,1)}, u32[]{:S(2)}, u32[]{:S(2)}) async-start(bf16[16,112,2048]{2,1,0:T(8,128)(2,1)} %bitcast.100), calls=%async_computation.1 | async-start | bytes 14680064 | tf_op jit(solution)/shard_map/all_to_all | solution.py:36
  226.3 155.7 %reduce-scatter.6.cloned.1.call-start = ((), (), s32[]{:S(2)}) async-start(), calls=%async_computation.6 | async-start | bytes 655360 | tf_op jit(solution)/shard_map/reduce_scatter | solution.py:102
  227.0 73.5 %copy-start.3 = (bf16[1,128,2048]{1,2,0:T(8,128)(2,1)}, bf16[1,128,2048]{1,2,0:T(8,128)(2,1)S(1)}, u32[]{:S(2)}) copy-start(bf16[1,128,2048]{1,2,0:T(8,128)(2,1)S(1)} %copy.60) | copy-start | bytes 1572868
  297.4 3.4 copy-start
  300.8 1.0 copy-start.4
  305.6 112.9 %reduce-scatter.8.cloned.1.call-start = ((), (), s32[]{:S(2)}) async-start(), calls=%async_computation.7 | async-start | bytes 655360 | tf_op jit(solution)/shard_map/reduce_scatter | solution.py:108
  311.5 125.7 %reduce-scatter.4.cloned.1.call-start = ((), (), s32[]{:S(2)}) async-start(), calls=%async_computation.5 | async-start | bytes 11010048 | tf_op jit(solution)/shard_map/reduce_scatter | solution.py:53
Sparse Core Ops, SparseCore 0:
  305.7 72.4 reduce-scatter.5
  381.8 36.6 reduce-scatter.7
  421.4 15.8 reduce-scatter.3
where the time goes:
time: 445 us; the launch traced here: 444 us
  waiting for transfers between devices  162 us (36%)
  local copies, waits for them, and re-layouts  127 us (29%)
  blocking collectives  66.8 us (15%)
  starting transfers between devices  39.4 us (9%)
  matrix products  32.1 us (7%)
  between operations  13.9 us (3%)
    all_to_all x1, waiting for transfers between devices, expert_grads(): lax.all_to_all(hidden_send.reshape(experts * shards, capacity, unit_piece...  57.2 us
    all_to_all x1, waiting for transfers between devices, expert_grads(): lax.all_to_all(grad_send.reshape(experts * shards, capacity, model_width)...  49.2 us
    all_gather x1, blocking collectives, attention_grads(): lax.all_gather(keys, 'seq', axis=1, tiled=True)  48.6 us
    scatter x2, local copies, waits for them, and re-layouts, expert_grads(): grad_send = grad_send.at[flat_ids, :, slot_index, :].set(spread)  46.5 us
    scatter x2, local copies, waits for them, and re-layouts, expert_grads(): hidden_send = hidden_send.at[flat_ids, :, slot_index, :].set(flat_hidden)  42.3 us
    reduce_scatter x1, waiting for transfers between devices, attention_grads(): lax.psum_scatter(value_part.reshape(1, key_count, KV_HEADS * HEAD_DIM).as...  36.6 us
    all_to_all x1, starting transfers between devices, expert_grads(): lax.all_to_all(grad_send.reshape(experts * shards, capacity, model_width)...  30.8 us
    dot_general x1, matrix products, expert_grads(): lax.dot_general(hidden_rows, grad_rows, (((0,), (0,)), ((), ())), preferr...  19.6 us
  transfers between devices with their start and end apart: 5, of which 4 were waited for; matrix products, arithmetic and copies ran while one was open for 23% of the time, Pallas kernels for 0%

commit v1 on v0

--- a/solution.py
+++ b/solution.py
@@ -6,6 +6,28 @@
 HEADS = 16
 KV_HEADS = 4
 HEAD_DIM = 128
+
+
+def split_up(x, dim, size):
+    before, after = (x.shape[:dim], x.shape[dim + 1 :])
+    return jnp.moveaxis(x.reshape(*before, size, -1, *after), dim, 0)
+
+
+def laid_out(blocks, dim):
+    shape = list(blocks.shape[1:])
+    shape[dim] *= blocks.shape[0]
+    return jnp.moveaxis(blocks, 0, dim).reshape(shape)
+
+
+def exchange_in_pairs(x, axis, split_dim, concat_dim):
+    length, place = (lax.axis_size(axis), lax.axis_index(axis))
+    blocks = split_up(x, split_dim, length)
+    outs = [blocks[place]]
+    for step in range(1, length):
+        sent = blocks[place ^ step]
+        outs.append(lax.ppermute(sent, axis, [(i, i ^ step) for i in range(length)]))
+    blocks = jnp.stack(outs)[place ^ jnp.arange(length)]
+    return laid_out(blocks, concat_dim)
 
 
 def expert_grads(grad_out, expert_ids, gate_weights, hidden):
@@ -40,12 +62,8 @@
             concat_axis=0,
             tiled=True,
         ),
-        lax.all_to_all(
-            hidden_send.reshape(experts * shards, capacity, unit_piece),
-            ("expert", "seq"),
-            split_axis=0,
-            concat_axis=0,
-            tiled=True,
+        exchange_in_pairs(
+            hidden_send.reshape(experts * shards, capacity, unit_piece), ("expert", "seq"), 0, 0
         ),
     )
     grad_rows = grad_recv.reshape(-1, model_width)

time: 445 us -> 489 us (1.099)
  starting transfers between devices: 39.4 us -> 76.8 us
  local copies, waits for them, and re-layouts: 127 us -> 155 us
  waiting for transfers between devices: 162 us -> 137 us
    ppermute x0 -> x15, waiting for transfers between devices: none -> 77.4 us  [exchange_in_pairs(): lax.ppermute(sent, axis, [(i, i ^ step) for i in range(length)])]
    ppermute x0 -> x15, starting transfers between devices: none -> 68 us  [exchange_in_pairs(): lax.ppermute(sent, axis, [(i, i ^ step) for i in range(length)])]
    all_to_all x1 -> x0, waiting for transfers between devices: 57.2 us -> none  [expert_grads(): lax.all_to_all(hidden_send.reshape(experts * shards, capacity, unit_piece...]
    all_to_all x1, waiting for transfers between devices: 49.2 us -> 0.01 us  [expert_grads(): lax.all_to_all(grad_send.reshape(experts * shards, capacity, model_width)...]
    reduce_scatter x1, waiting for transfers between devices: 18.7 us -> 59.8 us  [expert_grads(): lax.psum_scatter(lax.dot_general(hidden_rows, grad_rows, (((0,), (0,)), (...]
    reduce_scatter x1, waiting for transfers between devices: 36.6 us -> 0.01 us  [attention_grads(): lax.psum_scatter(value_part.reshape(1, key_count, KV_HEADS * HEAD_DIM).as...]
    all_to_all x1, starting transfers between devices: 30.8 us -> 8.48 us  [expert_grads(): lax.all_to_all(grad_send.reshape(experts * shards, capacity, model_width)...]
    unnamed x21 -> x41, local copies, waits for them, and re-layouts: 2.77 us -> 17.6 us
  transfers between devices with their start and end apart: 5 -> 19, of which waited for: 4 -> 9; matrix products, arithmetic and copies ran while one was open for 23% -> 25% of each run, Pallas kernels for 0% -> 0%
where the time goes in v1:
time: 489 us; the launch traced here: 488 us
  local copies, waits for them, and re-layouts  155 us (32%)
  waiting for transfers between devices  137 us (28%)
  starting transfers between devices  76.8 us (16%)
  blocking collectives  71 us (15%)
  matrix products  30 us (6%)
  between operations  14.1 us (3%)
    ppermute x15, waiting for transfers between devices, exchange_in_pairs(): lax.ppermute(sent, axis, [(i, i ^ step) for i in range(length)])  77.4 us
    ppermute x15, starting transfers between devices, exchange_in_pairs(): lax.ppermute(sent, axis, [(i, i ^ step) for i in range(length)])  68 us
    reduce_scatter x1, waiting for transfers between devices, expert_grads(): lax.psum_scatter(lax.dot_general(hidden_rows, grad_rows, (((0,), (0,)), (...  59.8 us
    all_gather x1, blocking collectives, attention_grads(): lax.all_gather(keys, 'seq', axis=1, tiled=True)  49.9 us
    scatter x2, local copies, waits for them, and re-layouts, expert_grads(): grad_send = grad_send.at[flat_ids, :, slot_index, :].set(spread)  46.5 us
    scatter x2, local copies, waits for them, and re-layouts, expert_grads(): hidden_send = hidden_send.at[flat_ids, :, slot_index, :].set(flat_hidden)  42.4 us
    all_gather x1, blocking collectives, attention_grads(): lax.all_gather(values, 'seq', axis=1, tiled=True)  21.2 us
    dot_general x1, matrix products, expert_grads(): lax.dot_general(hidden_rows, grad_rows, (((0,), (0,)), ((), ())), preferr...  19.6 us
  transfers between devices with their start and end apart: 19, of which 9 were waited for; matrix products, arithmetic and copies ran while one was open for 25% of the time, Pallas kernels for 0%

profile of v1, /device:TPU:0, one launch (start us, length us, event | category | flops | bytes accessed | tf_op | source)
XLA Modules:
  0.0 487.8 jit_solution(14571326137381581391)
XLA Ops:
  21.1 6.7 %broadcast_in_dim.7 = bf16[4,4,112,2048]{3,1,2,0:T(4,128)(2,1)} broadcast(bf16[]{:T(256)} %constant.24.clone.1), dimensions={} | broadcast | bytes 7340034 | tf_op jit(solution)/shard_map/broadcast_in_dim | solution.py:55
  27.8 36.3 %scatter_fusion.1 = bf16[4,4,112,2048]{3,1,2,0:T(4,128)(2,1)} fusion(bf16[4,4,112,2048]{3,1,2,0:T(4,128)(2,1)} %broadcast_in_dim.7, s32[256]{0:T(256)S(1)} %bitcast.161, bf16[256,4,2048]{2,1,0:T(4,128)(2,1)} %broadcast_in_dim.8), kind=kCustom, calls=%fused_computation.2 | custom fusion | bytes 12584960 | tf_op jit(solution)/shard_map/scatter | solution.py:56
  64.1 10.2 %copy.31 = bf16[4,4,112,2048]{3,2,1,0:T(8,128)(2,1)} copy(bf16[4,4,112,2048]{3,1,2,0:T(4,128)(2,1)} %scatter_fusion.1) | data formatting | bytes 14680064 | tf_op jit(solution)/shard_map/scatter | solution.py:56
  74.3 8.5 %all-to-all-start = ((bf16[16,112,2048]{2,1,0:T(8,128)(2,1)}), bf16[16,112,2048]{2,1,0:T(8,128)(2,1)}, u32[]{:S(2)}, u32[]{:S(2)}) async-start(bf16[16,112,2048]{2,1,0:T(8,128)(2,1)} %bitcast.163), calls=%async_computation | async-start | bytes 14680064 | tf_op jit(solution)/shard_map/all_to_all | solution.py:58
  83.7 49.9 %all_gather.6 = bf16[1,512,512]{1,2,0:T(8,128)(2,1)S(1)} all-gather(bf16[1,128,512]{1,2,0:T(8,128)(2,1)S(1)} %copy.32), channel_id=1, replica_groups=mesh['expert'=4,'seq'=4,'dp'=2] {'seq'}, dimensions={1}, use_global_device_ids=true | all-gather | bytes 655360 | tf_op jit(solution)/shard_map/all_gather | solution.py:87
  133.6 21.2 %all_gather.7 = bf16[1,512,512]{1,2,0:T(8,128)(2,1)S(1)} all-gather(bf16[1,128,512]{1,2,0:T(8,128)(2,1)S(1)} %copy.35), channel_id=1, replica_groups=mesh['expert'=4,'seq'=4,'dp'=2] {'seq'}, dimensions={1}, use_global_device_ids=true | all-gather | bytes 655360 | tf_op jit(solution)/shard_map/all_gather | solution.py:88
  166.3 9.8 %reshape.187 = bf16[256,4,1792]{2,1,0:T(4,128)(2,1)} reshape(bf16[1,128,2,7168]{3,2,1,0:T(2,128)(2,1)} %param.10) | data formatting | bytes 7340032 | tf_op jit(solution)/shard_map/reshape | solution.py:51
  176.1 4.3 broadcast_in_dim.6
  180.4 36.0 %scatter_fusion = bf16[4,4,112,1792]{3,1,2,0:T(4,128)(2,1)} fusion(bf16[4,4,112,1792]{3,1,2,0:T(4,128)(2,1)} %broadcast_in_dim.6, s32[256]{0:T(256)S(1)} %bitcast.162, bf16[256,4,1792]{2,1,0:T(4,128)(2,1)} %reshape.187), kind=kCustom, calls=%fused_computation.1 | custom fusion | bytes 11012096 | tf_op jit(solution)/shard_map/scatter | solution.py:53
  216.4 6.4 %copy.29 = bf16[4,4,112,1792]{3,2,1,0:T(8,128)(2,1)} copy(bf16[4,4,112,1792]{3,1,2,0:T(4,128)(2,1)} %scatter_fusion) | data formatting | bytes 12845056 | tf_op jit(solution)/shard_map/scatter | solution.py:53
  222.8 5.7 %dynamic-slice_bitcast_fusion = (bf16[1,112,1792]{2,1,0:T(8,128)(2,1)}, bf16[1,112,1792]{2,1,0:T(8,128)(2,1)}, bf16[1,112,1792]{2,1,0:T(8,128)(2,1)}, bf16[1,112...) fusion(bf16[16,1,112,1792]{3,2,0,1:T(8,128)(2,1)} %bitcast.164,, ...), kind=kLoop, calls=%fused_computation.43 | loop fusion | bytes 12845120 | tf_op jit(solution)/shard_map/squeeze | solution.py:27
  228.5 26.9 %collective-permute-start = (bf16[1,112,1792]{2,1,0:T(8,128)(2,1)}, bf16[1,112,1792]{2,1,0:T(8,128)(2,1)}, u32[]{:S(2)}, u32[]{:S(2)}) collective-permute-start(bf16[1,112,1792]{2,1,0:T(8,128)(2,1)} %get-tuple-element.26), channel_id=1, source_target_pairs={{0,2},{2,0},{4,6},{6,4},{8,10},{10,8},{12,14},{14,12},{16,18},{18,... | collective-permute-start | bytes 1204232 | tf_op jit(solution)/shard_map/ppermute | solution.py:28
  275.7 8.2 %collective-permute-done.2 = bf16[1,112,1792]{2,1,0:T(8,128)(2,1)} collective-permute-done((bf16[1,112,1792]{2,1,0:T(8,128)(2,1)}, bf16[1,112,1792]{2,1,0:T(8,128)(2,1)}, u32[]{:S(2)}, u32[]{:S(2)}) %collective-permute-start.2) | collective-permute-done | bytes 401440 | tf_op jit(solution)/shard_map/ppermute | solution.py:28
  285.7 11.9 %collective-permute-start.8 = (bf16[1,112,1792]{2,1,0:T(8,128)(2,1)}, bf16[1,112,1792]{2,1,0:T(8,128)(2,1)S(1)}, u32[]{:S(2)}, u32[]{:S(2)}) collective-permute-start(bf16[1,112,1792]{2,1,0:T(8,128)(2,1)} %get-tuple-element.18), channel_id=1, source_target_pairs={{0,18},{2,16},{4,22},{6,20},{8,26},{10,24},{12,30},{14,28},{16,2},... | collective-permute-start | bytes 1204232 | tf_op jit(solution)/shard_map/ppermute | solution.py:28
  300.1 5.4 %collective-permute-done.5 = bf16[1,112,1792]{2,1,0:T(8,128)(2,1)S(1)} collective-permute-done((bf16[1,112,1792]{2,1,0:T(8,128)(2,1)}, bf16[1,112,1792]{2,1,0:T(8,128)(2,1)S(1)}, u32[]{:S(2)}, u32[]{:S(2)}) %collective-permute-start.5) | collective-permute-done | bytes 401440 | tf_op jit(solution)/shard_map/ppermute | solution.py:28
  306.3 6.3 %collective-permute-done.6 = bf16[1,112,1792]{2,1,0:T(8,128)(2,1)S(1)} collective-permute-done((bf16[1,112,1792]{2,1,0:T(8,128)(2,1)}, bf16[1,112,1792]{2,1,0:T(8,128)(2,1)S(1)}, u32[]{:S(2)}, u32[]{:S(2)}) %collective-permute-start.6) | collective-permute-done | bytes 401440 | tf_op jit(solution)/shard_map/ppermute | solution.py:28
  313.4 26.8 %collective-permute-done.7 = bf16[1,112,1792]{2,1,0:T(8,128)(2,1)S(1)} collective-permute-done((bf16[1,112,1792]{2,1,0:T(8,128)(2,1)}, bf16[1,112,1792]{2,1,0:T(8,128)(2,1)S(1)}, u32[]{:S(2)}, u32[]{:S(2)}) %collective-permute-start.7) | collective-permute-done | bytes 401440 | tf_op jit(solution)/shard_map/ppermute | solution.py:28
  340.9 15.0 %collective-permute-done.8 = bf16[1,112,1792]{2,1,0:T(8,128)(2,1)S(1)} collective-permute-done((bf16[1,112,1792]{2,1,0:T(8,128)(2,1)}, bf16[1,112,1792]{2,1,0:T(8,128)(2,1)S(1)}, u32[]{:S(2)}, u32[]{:S(2)}) %collective-permute-start.8) | collective-permute-done | bytes 401440 | tf_op jit(solution)/shard_map/ppermute | solution.py:28
  355.9 6.1 %collective-permute-start.13 = (bf16[1,112,1792]{2,1,0:T(8,128)(2,1)}, bf16[1,112,1792]{2,1,0:T(8,128)(2,1)S(1)}, u32[]{:S(2)}, u32[]{:S(2)}) collective-permute-start(bf16[1,112,1792]{2,1,0:T(8,128)(2,1)} %get-tuple-element.13), channel_id=1, source_target_pairs={{0,28},{2,30},{4,24},{6,26},{8,20},{10,22},{12,16},{14,18},{16,12}... | collective-permute-start | bytes 1204232 | tf_op jit(solution)/shard_map/ppermute | solution.py:28
  362.8 16.4 %collective-permute-start.14 = (bf16[1,112,1792]{2,1,0:T(8,128)(2,1)}, bf16[1,112,1792]{2,1,0:T(8,128)(2,1)S(1)}, u32[]{:S(2)}, u32[]{:S(2)}) collective-permute-start(bf16[1,112,1792]{2,1,0:T(8,128)(2,1)} %get-tuple-element.12), channel_id=1, source_target_pairs={{0,30},{2,28},{4,26},{6,24},{8,22},{10,20},{12,18},{14,16},{16,14}... | collective-permute-start | bytes 1204232 | tf_op jit(solution)/shard_map/ppermute | solution.py:28
  379.9 9.9 %collective-permute-done.10 = bf16[1,112,1792]{2,1,0:T(8,128)(2,1)S(1)} collective-permute-done((bf16[1,112,1792]{2,1,0:T(8,128)(2,1)}, bf16[1,112,1792]{2,1,0:T(8,128)(2,1)S(1)}, u32[]{:S(2)}, u32[]{:S(2)}) %collective-permute-start.10) | collective-permute-done | bytes 401440 | tf_op jit(solution)/shard_map/ppermute | solution.py:28
  393.8 6.5 %gather_fusion = bf16[16,112,1792]{2,1,0:T(8,128)(2,1)} fusion(bf16[16,112,1792]{2,1,0:T(8,128)(2,1)} %bitcast.165, s32[1024]{0:T(1024)S(1)} %pad_clamp_fusion), kind=kCustom, calls=%fused_computation | custom fusion | bytes 12845120 | tf_op jit(solution)/shard_map/gather | solution.py:29
  400.3 19.6 %convolution_convert_fusion = bf16[1792,2048]{1,0:T(8,128)(2,1)} fusion(bf16[1792,1792]{1,0:T(8,128)(2,1)} %bitcast.166, bf16[1792,2048]{1,0:T(8,128)(2,1)} %bitcast.40), kind=kOutput, calls=%fused_computation.4 | convolution fusion | flops 13157007360 | bytes 21102592 | tf_op jit(solution)/shard_map/dot_general | solution.py:72
  421.4 59.8 %reduce-scatter.4.cloned.1.call-done = bf16[896,2048]{1,0:T(8,128)(2,1)} async-done(((bf16[1792,2048]{1,0:T(8,128)(2,1)}), bf16[896,2048]{1,0:T(8,128)(2,1)}) %reduce-scatter.4.cloned.1.call-update) | async-done | bytes 3670032 | tf_op jit(solution)/shard_map/reduce_scatter | solution.py:71
  (102 shorter events, 60.3 us)
Async XLA Ops:
  7.2 9.2 %copy-start.10 = (f32[1,128,2]{1,2,0:T(2,128)S(1)}, f32[1,128,2]{1,2,0:T(2,128)}, u32[]{:S(2)}) copy-start(f32[1,128,2]{1,2,0:T(2,128)} %param.9) | copy-start | bytes 3076
  74.3 9.3 %copy-start.7 = (bf16[1,128,512]{2,1,0:T(8,128)(2,1)S(1)}, bf16[1,128,512]{2,1,0:T(8,128)(2,1)}, u32[]{:S(2)}) copy-start(bf16[1,128,512]{2,1,0:T(8,128)(2,1)} %param.13) | copy-start | bytes 393220
  74.3 326.0 %all-to-all-start = ((bf16[16,112,2048]{2,1,0:T(8,128)(2,1)}), bf16[16,112,2048]{2,1,0:T(8,128)(2,1)}, u32[]{:S(2)}, u32[]{:S(2)}) async-start(bf16[16,112,2048]{2,1,0:T(8,128)(2,1)} %bitcast.163), calls=%async_computation | async-start | bytes 14680064 | tf_op jit(solution)/shard_map/all_to_all | solution.py:58
  82.7 338.7 %reduce-scatter.6.cloned.1.call-start = ((), (), s32[]{:S(2)}) async-start(), calls=%async_computation.5 | async-start | bytes 655360 | tf_op jit(solution)/shard_map/reduce_scatter | solution.py:120
  83.6 77.8 %copy-start.4 = (bf16[1,128,2048]{1,2,0:T(8,128)(2,1)}, bf16[1,128,2048]{1,2,0:T(8,128)(2,1)S(1)}, u32[]{:S(2)}) copy-start(bf16[1,128,2048]{1,2,0:T(8,128)(2,1)S(1)} %copy.58) | copy-start | bytes 1572868
  166.2 255.2 %reduce-scatter.8.cloned.1.call-start = ((), (), s32[]{:S(2)}) async-start(), calls=%async_computation.6 | async-start | bytes 655360 | tf_op jit(solution)/shard_map/reduce_scatter | solution.py:126
  222.8 39.0 %copy-start.1 = (f32[4,4,128,512]{2,3,1,0:T(8,128)S(1)}, f32[4,4,128,512]{2,3,1,0:T(8,128)}, u32[]{:S(2)}) copy-start(f32[4,4,128,512]{2,3,1,0:T(8,128)} %get-tuple-element.29) | copy-start | bytes 12582916
  222.8 39.0 %copy-start.9 = (f32[4,4,128]{2,1,0:T(4,128)S(1)}, f32[4,4,128]{2,1,0:T(4,128)}, u32[]{:S(2)}) copy-start(f32[4,4,128]{2,1,0:T(4,128)} %copy-done.8) | copy-start | bytes 24580
  228.5 40.7 %collective-permute-start = (bf16[1,112,1792]{2,1,0:T(8,128)(2,1)}, bf16[1,112,1792]{2,1,0:T(8,128)(2,1)}, u32[]{:S(2)}, u32[]{:S(2)}) collective-permute-start(bf16[1,112,1792]{2,1,0:T(8,128)(2,1)} %get-tuple-element.26), channel_id=1, source_target_pairs={{0,2},{2,0},{4,6},{6,4},{8,10},{10,8},{12,14},{14,12},{16,18},{18,... | collective-permute-start | bytes 1204232 | tf_op jit(solution)/shard_map/ppermute | solution.py:28
  255.4 18.2 %collective-permute-start.1 = (bf16[1,112,1792]{2,1,0:T(8,128)(2,1)}, bf16[1,112,1792]{2,1,0:T(8,128)(2,1)}, u32[]{:S(2)}, u32[]{:S(2)}) collective-permute-start(bf16[1,112,1792]{2,1,0:T(8,128)(2,1)} %get-tuple-element.25), channel_id=1, source_target_pairs={{0,4},{2,6},{4,0},{6,2},{8,12},{10,14},{12,8},{14,10},{16,20},{18,... | collective-permute-start | bytes 1204232 | tf_op jit(solution)/shard_map/ppermute | solution.py:28
  258.4 25.4 %collective-permute-start.2 = (bf16[1,112,1792]{2,1,0:T(8,128)(2,1)}, bf16[1,112,1792]{2,1,0:T(8,128)(2,1)}, u32[]{:S(2)}, u32[]{:S(2)}) collective-permute-start(bf16[1,112,1792]{2,1,0:T(8,128)(2,1)} %get-tuple-element.24), channel_id=1, source_target_pairs={{0,6},{2,4},{4,2},{6,0},{8,14},{10,12},{12,10},{14,8},{16,22},{18,... | collective-permute-start | bytes 1204232 | tf_op jit(solution)/shard_map/ppermute | solution.py:28
  259.8 25.9 %collective-permute-start.3 = (bf16[1,112,1792]{2,1,0:T(8,128)(2,1)}, bf16[1,112,1792]{2,1,0:T(8,128)(2,1)}, u32[]{:S(2)}, u32[]{:S(2)}) collective-permute-start(bf16[1,112,1792]{2,1,0:T(8,128)(2,1)} %get-tuple-element.23), channel_id=1, source_target_pairs={{0,8},{2,10},{4,12},{6,14},{8,0},{10,2},{12,4},{14,6},{16,24},{18,... | collective-permute-start | bytes 1204232 | tf_op jit(solution)/shard_map/ppermute | solution.py:28
  259.8 39.5 %collective-permute-start.4 = (bf16[1,112,1792]{2,1,0:T(8,128)(2,1)}, bf16[1,112,1792]{2,1,0:T(8,128)(2,1)S(1)}, u32[]{:S(2)}, u32[]{:S(2)}) collective-permute-start(bf16[1,112,1792]{2,1,0:T(8,128)(2,1)} %get-tuple-element.22), channel_id=1, source_target_pairs={{0,10},{2,8},{4,14},{6,12},{8,2},{10,0},{12,6},{14,4},{16,26},{18,... | collective-permute-start | bytes 1204232 | tf_op jit(solution)/shard_map/ppermute | solution.py:28
  265.5 215.7 %reduce-scatter.4.cloned.1.call-start = ((), (), s32[]{:S(2)}) async-start(), calls=%async_computation.4 | async-start | bytes 11010048 | tf_op jit(solution)/shard_map/reduce_scatter | solution.py:71
  269.2 36.3 %collective-permute-start.5 = (bf16[1,112,1792]{2,1,0:T(8,128)(2,1)}, bf16[1,112,1792]{2,1,0:T(8,128)(2,1)S(1)}, u32[]{:S(2)}, u32[]{:S(2)}) collective-permute-start(bf16[1,112,1792]{2,1,0:T(8,128)(2,1)} %get-tuple-element.21), channel_id=1, source_target_pairs={{0,12},{2,14},{4,8},{6,10},{8,4},{10,6},{12,0},{14,2},{16,28},{18,... | collective-permute-start | bytes 1204232 | tf_op jit(solution)/shard_map/ppermute | solution.py:28
  273.6 39.0 %collective-permute-start.6 = (bf16[1,112,1792]{2,1,0:T(8,128)(2,1)}, bf16[1,112,1792]{2,1,0:T(8,128)(2,1)S(1)}, u32[]{:S(2)}, u32[]{:S(2)}) collective-permute-start(bf16[1,112,1792]{2,1,0:T(8,128)(2,1)} %get-tuple-element.20), channel_id=1, source_target_pairs={{0,14},{2,12},{4,10},{6,8},{8,6},{10,4},{12,2},{14,0},{16,30},{18,... | collective-permute-start | bytes 1204232 | tf_op jit(solution)/shard_map/ppermute | solution.py:28
  283.9 56.3 %collective-permute-start.7 = (bf16[1,112,1792]{2,1,0:T(8,128)(2,1)}, bf16[1,112,1792]{2,1,0:T(8,128)(2,1)S(1)}, u32[]{:S(2)}, u32[]{:S(2)}) collective-permute-start(bf16[1,112,1792]{2,1,0:T(8,128)(2,1)} %get-tuple-element.19), channel_id=1, source_target_pairs={{0,16},{2,18},{4,20},{6,22},{8,24},{10,26},{12,28},{14,30},{16,0},... | collective-permute-start | bytes 1204232 | tf_op jit(solution)/shard_map/ppermute | solution.py:28
  285.7 70.2 %collective-permute-start.8 = (bf16[1,112,1792]{2,1,0:T(8,128)(2,1)}, bf16[1,112,1792]{2,1,0:T(8,128)(2,1)S(1)}, u32[]{:S(2)}, u32[]{:S(2)}) collective-permute-start(bf16[1,112,1792]{2,1,0:T(8,128)(2,1)} %get-tuple-element.18), channel_id=1, source_target_pairs={{0,18},{2,16},{4,22},{6,20},{8,26},{10,24},{12,30},{14,28},{16,2},... | collective-permute-start | bytes 1204232 | tf_op jit(solution)/shard_map/ppermute | solution.py:28
  299.3 63.5 %collective-permute-start.9 = (bf16[1,112,1792]{2,1,0:T(8,128)(2,1)}, bf16[1,112,1792]{2,1,0:T(8,128)(2,1)S(1)}, u32[]{:S(2)}, u32[]{:S(2)}) collective-permute-start(bf16[1,112,1792]{2,1,0:T(8,128)(2,1)} %get-tuple-element.17), channel_id=1, source_target_pairs={{0,20},{2,22},{4,16},{6,18},{8,28},{10,30},{12,24},{14,26},{16,4},... | collective-permute-start | bytes 1204232 | tf_op jit(solution)/shard_map/ppermute | solution.py:28
  305.5 84.4 %collective-permute-start.10 = (bf16[1,112,1792]{2,1,0:T(8,128)(2,1)}, bf16[1,112,1792]{2,1,0:T(8,128)(2,1)S(1)}, u32[]{:S(2)}, u32[]{:S(2)}) collective-permute-start(bf16[1,112,1792]{2,1,0:T(8,128)(2,1)} %get-tuple-element.16), channel_id=1, source_target_pairs={{0,22},{2,20},{4,18},{6,16},{8,30},{10,28},{12,26},{14,24},{16,6},... | collective-permute-start | bytes 1204232 | tf_op jit(solution)/shard_map/ppermute | solution.py:28
  312.6 78.1 %collective-permute-start.11 = (bf16[1,112,1792]{2,1,0:T(8,128)(2,1)}, bf16[1,112,1792]{2,1,0:T(8,128)(2,1)S(1)}, u32[]{:S(2)}, u32[]{:S(2)}) collective-permute-start(bf16[1,112,1792]{2,1,0:T(8,128)(2,1)} %get-tuple-element.15), channel_id=1, source_target_pairs={{0,24},{2,26},{4,28},{6,30},{8,16},{10,18},{12,20},{14,22},{16,8},... | collective-permute-start | bytes 1204232 | tf_op jit(solution)/shard_map/ppermute | solution.py:28
  340.1 51.3 %collective-permute-start.12 = (bf16[1,112,1792]{2,1,0:T(8,128)(2,1)}, bf16[1,112,1792]{2,1,0:T(8,128)(2,1)S(1)}, u32[]{:S(2)}, u32[]{:S(2)}) collective-permute-start(bf16[1,112,1792]{2,1,0:T(8,128)(2,1)} %get-tuple-element.14), channel_id=1, source_target_pairs={{0,26},{2,24},{4,30},{6,28},{8,18},{10,16},{12,22},{14,20},{16,10}... | collective-permute-start | bytes 1204232 | tf_op jit(solution)/shard_map/ppermute | solution.py:28
  355.9 36.3 %collective-permute-start.13 = (bf16[1,112,1792]{2,1,0:T(8,128)(2,1)}, bf16[1,112,1792]{2,1,0:T(8,128)(2,1)S(1)}, u32[]{:S(2)}, u32[]{:S(2)}) collective-permute-start(bf16[1,112,1792]{2,1,0:T(8,128)(2,1)} %get-tuple-element.13), channel_id=1, source_target_pairs={{0,28},{2,30},{4,24},{6,26},{8,20},{10,22},{12,16},{14,18},{16,12}... | collective-permute-start | bytes 1204232 | tf_op jit(solution)/shard_map/ppermute | solution.py:28
  362.8 30.2 %collective-permute-start.14 = (bf16[1,112,1792]{2,1,0:T(8,128)(2,1)}, bf16[1,112,1792]{2,1,0:T(8,128)(2,1)S(1)}, u32[]{:S(2)}, u32[]{:S(2)}) collective-permute-start(bf16[1,112,1792]{2,1,0:T(8,128)(2,1)} %get-tuple-element.12), channel_id=1, source_target_pairs={{0,30},{2,28},{4,26},{6,24},{8,22},{10,20},{12,18},{14,16},{16,14}... | collective-permute-start | bytes 1204232 | tf_op jit(solution)/shard_map/ppermute | solution.py:28
  (6 other events, 34.1 us)
Sparse Core Ops, SparseCore 0:
  166.3 75.2 reduce-scatter.5
  265.7 42.6 reduce-scatter.7
  420.0 61.1 reduce-scatter.3
